TPU v7x, 32 devices: a whole 2x2x4 slice. The times are simulated.
32 devices in a mesh: group: 2 (over y), mrow: 4 (over z), mcol: 2 (over x), sub: 2 (over core).
Axes of the slice: x: 2, y: 2, z: 4, core: 2. Of those that a mesh axis runs over, the one named last changes fastest.
Arguments:
- tokens: bfloat16 [1024, 6144], P(('group', 'mrow'), ('mcol', 'sub')), parts along dimension 0, may hold values from -8 to 8
- ln_gain: float32 [6144], P(('mcol', 'sub')), may hold values from 0.1 to 1.9
- w_in: bfloat16 [6144, 24576], P(('mcol', 'sub'), 'mrow'), may hold values from -0.078125 to 0.078125
- b_in: float32 [24576], P('mrow'), may hold values from -3 to 3
- w_out: bfloat16 [24576, 6144], P('mrow', ('mcol', 'sub')), may hold values from -0.0390625 to 0.0390625
- b_out: float32 [6144], replicated, may hold values from -0.6 to 0.6
- captions: bfloat16 [2048, 6144], P(('group', 'mrow', 'mcol', 'sub')), parts along dimension 0, may hold values from -6 to 6
- pairs: int32 [2048], P(('group', 'mrow', 'mcol', 'sub')), parts along dimension 0, may hold values from 0 to 1
Outputs:
- scores: float32 [2048], P(('group', 'mrow', 'mcol', 'sub')), parts along dimension 0
There are 2 independent parts, one for each index of `group`. A program takes and returns all parts, laid end to end along the dimension named above; an argument that names none is the same for every part. Nothing has to cross between parts.
All inputs are finite; a program needn't handle non-finite values.
Results may differ from a plain program's by a relative error of at most 0.0065.
Values may be sent and summed in bfloat16 or wider, within the bound.
A program may use at most 128 MiB of HBM per device.

v0:
```python
import functools

import jax
import jax.numpy as jnp
from jax import lax
from jax.experimental import pallas as pl
from jax.experimental.pallas import tpu as pltpu
from jax.sharding import PartitionSpec as P

MESH = pl.DeviceIdType.MESH

D = 6144
PATCHES = 256
IMAGES = 2


def image_table(first_row, count):
    positions = first_row + jnp.arange(count, dtype=jnp.int32)
    return (positions[None, :] // PATCHES == jnp.arange(IMAGES, dtype=jnp.int32)[:, None]).astype(
        jnp.bfloat16
    )


def plain(tokens, ln_gain, w_in, b_in, w_out, b_out, captions, pairs):
    values = tokens.astype(jnp.float32)
    totals, squares = lax.psum(
        (jnp.sum(values, axis=1), jnp.sum(values * values, axis=1)), ("mcol", "sub")
    )
    average = totals / D
    variance = squares / D - average * average
    normed = (
        (values - average[:, None]) * lax.rsqrt(variance + 1e-06)[:, None] * ln_gain[None, :]
    ).astype(jnp.bfloat16)
    gathered = lax.all_gather(normed, "mrow", axis=0, tiled=True)
    rows_local = tokens.shape[0]
    columns = tokens.shape[1]
    col_index = lax.axis_index(("mcol", "sub"))
    row_index = lax.axis_index("mrow")
    resid_pool = jnp.dot(
        image_table(row_index * rows_local, rows_local), tokens, preferred_element_type=jnp.float32
    )
    empty = jnp.zeros((IMAGES, D), jnp.float32)
    offset = col_index * columns
    out_weights = w_out.astype(jnp.float32)
    full_preact = jnp.dot(gathered, w_in, preferred_element_type=jnp.float32)
    preact = lax.psum_scatter(
        full_preact.astype(jnp.bfloat16), ("mcol", "sub"), scatter_dimension=1, tiled=True
    ).astype(jnp.float32)
    units = preact.shape[1]
    unit_bias = lax.dynamic_slice_in_dim(b_in, col_index * units, units, 0)
    hidden = jax.nn.gelu(preact + unit_bias[None, :], approximate=True).astype(jnp.bfloat16)
    local_pool = jnp.dot(
        image_table(0, hidden.shape[0]), hidden, preferred_element_type=jnp.float32
    )
    pooled_hidden = lax.all_gather(local_pool, ("mcol", "sub"), axis=1, tiled=True) / PATCHES
    mixed = jnp.dot(pooled_hidden, out_weights, precision=lax.Precision.HIGHEST)
    placed = lax.dynamic_update_slice(empty, resid_pool / PATCHES + mixed, (0, offset))
    pooled = lax.psum(placed, ("mrow", "mcol", "sub")) + b_out[None, :]
    embedding = (
        pooled * lax.rsqrt(jnp.mean(pooled * pooled, axis=1, keepdims=True) + 1e-06)
    ).astype(jnp.bfloat16)
    similar = jnp.dot(captions, embedding.T, preferred_element_type=jnp.float32)
    chosen = pairs[:, None] == jnp.arange(IMAGES, dtype=jnp.int32)[None, :]
    picked = jnp.sum(jnp.where(chosen, similar, 0.0), axis=1)
    text_vals = captions.astype(jnp.float32)
    text_scale = lax.rsqrt(jnp.mean(text_vals * text_vals, axis=1) + 1e-06)
    return 100.0 * picked * text_scale / D


def column_tile(width):
    return next(t for t in (1536, 768, 512, 384, 256, 128) if width % t == 0)


def kernel(
    sizes,
    tokens_hbm, gain_ref, w_in_hbm, b_in_ref, w_out_hbm, b_out_ref, captions_hbm, pairs_ref,
    out_ref,
    x_all, normed, w_in_v, w_out_v, captions_v, to_sub, from_sub, kept, to_col, from_col, own,
    stats, row_stats, pool_all, mixed_all, pooled_all,
    local_sem, w_sem,
    z_send, z_recv, stat_send, stat_recv, rows_send, rows_recv,
    sub_send, sub_recv, col_send, col_recv,
    pool_send, pool_recv, mixed_send, mixed_recv, pooled_send, pooled_recv,
):
    n_r, n_c, n_s = sizes
    n_q = n_c * n_s
    g = lax.axis_index("group")
    r = lax.axis_index("mrow")
    c = lax.axis_index("mcol")
    s = lax.axis_index("sub")
    q = c * n_s + s
    rows, depth = x_all.shape[1], x_all.shape[2]
    units = own.shape[2]
    features = depth * n_q
    oc, os = 1 - c, 1 - s

    def peer_q(k):
        other = lax.rem(q + k, n_q)
        return other, (g, r, lax.div(other, n_s), lax.rem(other, n_s))

    def peer_r(k):
        other = lax.rem(r + k, n_r)
        return other, (g, other, c, s)

    quarters = (oc * n_s + os, oc * n_s + s, c * n_s + os, c * n_s + s)

    ut = column_tile(units)
    tiles = units // ut

    def tile_at(t):
        return pl.ds(pl.multiple_of(t * ut, 128), ut)

    def w_in_copy(j, t):
        start = pl.multiple_of(quarters[j] * units + t * ut, 128)
        return pltpu.make_async_copy(
            w_in_hbm.at[:, pl.ds(start, ut)], w_in_v.at[j, :, tile_at(t)], w_sem.at[j, t])

    tokens_copy = pltpu.make_async_copy(tokens_hbm, x_all.at[r], local_sem.at[0])
    w_out_copy = pltpu.make_async_copy(w_out_hbm, w_out_v, local_sem.at[1])
    captions_copy = pltpu.make_async_copy(captions_hbm, captions_v, local_sem.at[2])
    tokens_copy.start()
    for pair in (0, 2):
        for t in range(tiles):
            w_in_copy(pair, t).start()
            w_in_copy(pair + 1, t).start()

    barrier = pltpu.get_barrier_semaphore()
    for k in range(1, n_q):
        pl.semaphore_signal(barrier, inc=1, device_id=peer_q(k)[1], device_id_type=MESH)
    for k in range(1, n_r):
        pl.semaphore_signal(barrier, inc=1, device_id=peer_r(k)[1], device_id_type=MESH)
    tokens_copy.wait()

    ct = column_tile(depth)
    total = jnp.zeros((rows, 1), jnp.float32)
    squares = jnp.zeros((rows, 1), jnp.float32)
    row_id = lax.broadcasted_iota(jnp.int32, (IMAGES, 1), 0)
    image = lax.div(r * rows, PATCHES)
    resid = []
    for start in range(0, depth, ct):
        part = x_all[r, :, start : start + ct].astype(jnp.float32)
        total += jnp.sum(part, axis=1, keepdims=True)
        squares += jnp.sum(part * part, axis=1, keepdims=True)
        resid.append(jnp.sum(part, axis=0, keepdims=True))
    mixed_all[r] = jnp.where(row_id == image, jnp.concatenate(resid, axis=1), 0.0) / PATCHES
    lane = lax.broadcasted_iota(jnp.int32, (rows, 128), 1)
    both = jnp.where(lane == 0, total, jnp.where(lane == 1, squares, 0.0))
    stats[q] = jnp.transpose(both)[:8, :]

    pl.semaphore_wait(barrier, n_q - 1 + n_r - 1)

    def stat_copy(k, slot):
        return pltpu.make_async_remote_copy(
            src_ref=stats.at[q], dst_ref=stats.at[q], send_sem=stat_send.at[k],
            recv_sem=stat_recv.at[slot], device_id=peer_q(k)[1], device_id_type=MESH)

    for k in range(1, n_q):
        stat_copy(k, q).start()

    def relay(way, distance, block):
        towards = r + 1 if way == 0 else r - 1
        return pltpu.make_async_remote_copy(
            src_ref=x_all.at[block], dst_ref=x_all.at[block], send_sem=z_send.at[way, distance],
            recv_sem=z_recv.at[way, distance + 1], device_id=(g, towards, c, s), device_id_type=MESH)

    def relay_arrival(way, distance, block):
        return pltpu.make_async_remote_copy(
            src_ref=x_all.at[block], dst_ref=x_all.at[block], send_sem=z_send.at[way, 0],
            recv_sem=z_recv.at[way, distance], device_id=(g, r, c, s), device_id_type=MESH)

    def forward(way, distance, block):
        @pl.when(r + 1 < n_r if way == 0 else r > 0)
        def _():
            relay(way, distance, block).start()

    forward(0, 0, r)
    forward(1, 0, r)

    for k in range(1, n_q):
        other, _ = peer_q(k)
        pltpu.make_async_remote_copy(
            src_ref=stats.at[other], dst_ref=stats.at[other], send_sem=stat_send.at[k],
            recv_sem=stat_recv.at[other], device_id=peer_q(k)[1], device_id_type=MESH).wait_recv()
    summed = stats[0]
    for k in range(1, n_q):
        summed = summed + stats[k]
    average = summed[0:1, :] / features
    variance = summed[1:2, :] / features - average * average
    spread = lax.rsqrt(variance + 1e-06)
    first = lax.broadcasted_iota(jnp.int32, (8, rows), 0) == 0
    row_stats[r] = jnp.where(first, average, spread)

    def rows_copy(k, slot):
        return pltpu.make_async_remote_copy(
            src_ref=row_stats.at[slot], dst_ref=row_stats.at[slot], send_sem=rows_send.at[k],
            recv_sem=rows_recv.at[slot], device_id=peer_r(k)[1], device_id_type=MESH)

    for k in range(1, n_r):
        rows_copy(k, r).start()

    partner = (g, r, c, os)
    across = (g, r, oc, s)

    def sub_copy(block, half, t):
        return pltpu.make_async_remote_copy(
            src_ref=to_sub.at[block, half, :, tile_at(t)],
            dst_ref=from_sub.at[block, half, :, tile_at(t)],
            send_sem=sub_send.at[block, half, t], recv_sem=sub_recv.at[block, half, t],
            device_id=partner, device_id_type=MESH)

    def col_copy(block, t):
        return pltpu.make_async_remote_copy(
            src_ref=to_col.at[block, :, tile_at(t)], dst_ref=from_col.at[block, :, tile_at(t)],
            send_sem=col_send.at[block, t], recv_sem=col_recv.at[block, t],
            device_id=across, device_id_type=MESH)

    def over_tiles(width, tile, body):
        def step(i, carry):
            body(pl.ds(pl.multiple_of(i * tile, 128), tile))
            return carry

        lax.fori_loop(0, width // tile, step, 0)

    def product(j, cols):
        return jnp.dot(normed[...], w_in_v[j, :, cols], preferred_element_type=jnp.float32)

    def process(block, mine, midway):
        @pl.when(jnp.logical_not(mine))
        def _():
            pltpu.make_async_remote_copy(
                src_ref=row_stats.at[block], dst_ref=row_stats.at[block], send_sem=rows_send.at[0],
                recv_sem=rows_recv.at[block], device_id=(g, block, c, s),
                device_id_type=MESH).wait_recv()

        columns = jnp.transpose(jnp.concatenate([row_stats[block]] * 16, axis=0))
        mean_col, spread_col = columns[:, 0:1], columns[:, 1:2]

        def normalise(cols):
            values = x_all[block, :, cols].astype(jnp.float32)
            normed[:, cols] = (
                (values - mean_col) * spread_col * gain_ref[cols][None, :]
            ).astype(jnp.bfloat16)

        over_tiles(depth, ct, normalise)

        def ready(j, t):
            @pl.when(mine)
            def _():
                w_in_copy(j, t).wait()

        def chip_sum(t):
            cols = tile_at(t)
            sub_copy(block, 0, t).wait_recv()
            to_col[block, :, cols] = (
                kept[:, cols] + from_sub[block, 0, :, cols].astype(jnp.float32)
            ).astype(jnp.bfloat16)
            col_copy(block, t).start()

        def sent_quarters(t, carry):
            cols = tile_at(t)
            ready(0, t)
            to_sub[block, 0, :, cols] = product(0, cols).astype(jnp.bfloat16)
            sub_copy(block, 0, t).start()
            ready(1, t)
            kept[:, cols] = product(1, cols)

            @pl.when(t > 0)
            def _():
                chip_sum(t - 1)

            return carry

        def own_quarters(t, carry):
            cols = tile_at(t)
            ready(2, t)
            to_sub[block, 1, :, cols] = product(2, cols).astype(jnp.bfloat16)
            sub_copy(block, 1, t).start()

            @pl.when(t == 0)
            def _():
                chip_sum(tiles - 1)

            ready(3, t)
            own[block, :, cols] = product(3, cols)
            return carry

        lax.fori_loop(0, tiles, sent_quarters, 0)
        midway()
        lax.fori_loop(0, tiles, own_quarters, 0)

        @pl.when(mine)
        def _():
            w_out_copy.start()
            captions_copy.start()

    def receive(distance):
        @pl.when(r - distance >= 0)
        def _():
            relay_arrival(0, distance, r - distance).wait_recv()
            forward(0, distance, r - distance)

        @pl.when(r + distance < n_r)
        def _():
            relay_arrival(1, distance, r + distance).wait_recv()
            forward(1, distance, r + distance)

    def at_distance(distance, carry):
        last = (r == 0) | (r + 1 == n_r)

        @pl.when((distance == 1) | ((distance > 1) & last))
        def _():
            receive(distance)

        def side(which, inner):
            block = r + distance * (2 * which - 1)
            valid = (block >= 0) & (block < n_r) & ((distance > 0) | (which == 0))

            def midway():
                nearest = (which == 1) | (r + distance >= n_r)

                @pl.when((distance > 0) & nearest & jnp.logical_not(last))
                def _():
                    receive(distance + 1)

            @pl.when(valid)
            def _():
                process(block, distance == 0, midway)

            return inner

        lax.fori_loop(0, 2, side, 0)
        return carry

    lax.fori_loop(0, n_r, at_distance, 0)

    captions_copy.wait()
    n_caps = captions_v.shape[0]
    norms = jnp.zeros((n_caps, 1), jnp.float32)
    for start in range(0, features, ct):
        part = captions_v[:, start : start + ct].astype(jnp.float32)
        norms += jnp.sum(part * part, axis=1, keepdims=True)
    text_scale = lax.rsqrt(norms / features + 1e-06)
    text_row = jnp.transpose(jnp.broadcast_to(text_scale, (n_caps, 128)))[0:1, :]

    bias_at = pl.multiple_of(q * units, 128)
    pool_all[q] = jnp.zeros((IMAGES, units), jnp.float32)

    def finish(block):
        image_mask = row_id == lax.div(block * rows, PATCHES)

        def body(i, carry):
            at = pl.multiple_of(i * ut, 128)
            cols = pl.ds(at, ut)
            sub_copy(block, 1, i).wait_recv()
            col_copy(block, i).wait_recv()
            v = (
                own[block, :, cols]
                + from_sub[block, 1, :, cols].astype(jnp.float32)
                + from_col[block, :, cols].astype(jnp.float32)
                + b_in_ref[:, pl.ds(pl.multiple_of(bias_at + at, 128), ut)]
            )
            inner = 0.7978845608028654 * (v + 0.044715 * (v * v * v))
            hidden = (0.5 * v * (1.0 + jnp.tanh(inner))).astype(jnp.bfloat16)
            sums = jnp.sum(hidden.astype(jnp.float32), axis=0, keepdims=True)
            pool_all[q, :, cols] += jnp.where(image_mask, sums, 0.0)
            return carry

        lax.fori_loop(0, tiles, body, 0)

    def finish_distance(distance, carry):
        def side(which, inner):
            block = r + distance * (2 * which - 1)
            valid = (block >= 0) & (block < n_r) & ((distance > 0) | (which == 0))

            @pl.when(valid)
            def _():
                finish(block)

            return inner

        lax.fori_loop(0, 2, side, 0)
        return carry

    lax.fori_loop(0, n_r, finish_distance, 0)

    def q_copy(ref, send, recv, k, slot):
        return pltpu.make_async_remote_copy(
            src_ref=ref.at[slot], dst_ref=ref.at[slot], send_sem=send.at[k],
            recv_sem=recv.at[slot], device_id=peer_q(k)[1], device_id_type=MESH)

    for k in range(1, n_q):
        q_copy(pool_all, pool_send, pool_recv, k, q).start()
    w_out_copy.wait()
    acc = jnp.zeros((8, depth), jnp.float32)
    for k in range(n_q):
        other, _ = peer_q(k)
        if k:
            q_copy(pool_all, pool_send, pool_recv, k, other).wait_recv()
        value = pool_all[other] / PATCHES
        high = value.astype(jnp.bfloat16).astype(jnp.float32)
        rest = value - high
        middle = rest.astype(jnp.bfloat16).astype(jnp.float32)
        low = rest - middle
        terms = jnp.concatenate(
            [high, middle, low, jnp.zeros((8 - 3 * IMAGES, units), jnp.float32)], axis=0
        ).astype(jnp.bfloat16)
        at = pl.ds(pl.multiple_of(other * units, 128), units)
        acc = acc + jnp.dot(terms, w_out_v[at, :], preferred_element_type=jnp.float32)
    mixed_all[r] = mixed_all[r] + (
        acc[0:IMAGES] + acc[IMAGES : 2 * IMAGES] + acc[2 * IMAGES : 3 * IMAGES]
    )

    def mixed_copy(k, slot):
        return pltpu.make_async_remote_copy(
            src_ref=mixed_all.at[slot], dst_ref=mixed_all.at[slot], send_sem=mixed_send.at[k],
            recv_sem=mixed_recv.at[slot], device_id=peer_r(k)[1], device_id_type=MESH)

    for k in range(1, n_r):
        mixed_copy(k, r).start()
    for k in range(1, n_r):
        mixed_copy(k, peer_r(k)[0]).wait_recv()
    pooled = b_out_ref[:, pl.ds(pl.multiple_of(q * depth, 128), depth)] + mixed_all[0]
    for k in range(1, n_r):
        pooled = pooled + mixed_all[k]
    pooled_all[q] = pooled
    for k in range(1, n_q):
        q_copy(pooled_all, pooled_send, pooled_recv, k, q).start()
    for k in range(1, n_q):
        q_copy(pooled_all, pooled_send, pooled_recv, k, peer_q(k)[0]).wait_recv()
    power = jnp.zeros((IMAGES, 1), jnp.float32)
    for k in range(n_q):
        power += jnp.sum(pooled_all[k] * pooled_all[k], axis=1, keepdims=True)
    scale = lax.rsqrt(power / features + 1e-06)
    similar = jnp.zeros((IMAGES, n_caps), jnp.float32)
    for k in range(n_q):
        embedding = (pooled_all[k] * scale).astype(jnp.bfloat16)
        similar += lax.dot_general(
            embedding, captions_v[:, k * depth : (k + 1) * depth],
            (((1,), (1,)), ((), ())), preferred_element_type=jnp.float32)
    chosen = pairs_ref[...] == lax.broadcasted_iota(jnp.int32, (IMAGES, n_caps), 0)
    picked = jnp.sum(jnp.where(chosen, similar, 0.0), axis=0, keepdims=True)
    out_ref[...] = 100.0 * picked * text_row / features

    for k in range(1, n_q):
        stat_copy(k, q).wait_send()
        q_copy(pool_all, pool_send, pool_recv, k, q).wait_send()
        q_copy(pooled_all, pooled_send, pooled_recv, k, q).wait_send()
    for k in range(1, n_r):
        rows_copy(k, r).wait_send()
        mixed_copy(k, r).wait_send()

    def drain(block, carry):
        for t in range(tiles):
            sub_copy(block, 0, t).wait_send()
            sub_copy(block, 1, t).wait_send()
            col_copy(block, t).wait_send()

        @pl.when((block <= r) & (r + 1 < n_r))
        def _():
            relay(0, r - block, block).wait_send()

        @pl.when((block >= r) & (r > 0))
        def _():
            relay(1, block - r, block).wait_send()

        return carry

    lax.fori_loop(0, n_r, drain, 0)


def shards(shape, tokens, ln_gain, w_in, b_in, w_out, b_out, captions, pairs):
    n_r, n_c, n_s = shape["mrow"], shape["mcol"], shape["sub"]
    n_q = n_c * n_s
    rows, depth = tokens.shape
    units = w_in.shape[1] // n_q
    n_caps, features = captions.shape
    fits = (
        n_c == 2 and n_s == 2 and n_r > 1 and rows % 128 == 0 and PATCHES % rows == 0
        and depth % 128 == 0 and units % 128 == 0 and n_caps % 8 == 0
        and rows * n_r == IMAGES * PATCHES
    )
    if not fits:
        return plain(tokens, ln_gain, w_in, b_in, w_out, b_out, captions, pairs)
    tiles = units // column_tile(units)
    bf16, f32 = jnp.bfloat16, jnp.float32
    any_spec = pl.BlockSpec(memory_space=pl.ANY)
    vmem = pl.BlockSpec(memory_space=pltpu.VMEM)
    dma = pltpu.SemaphoreType.DMA
    result = pl.pallas_call(
        functools.partial(kernel, (n_r, n_c, n_s)),
        out_shape=jax.ShapeDtypeStruct((1, n_caps), f32),
        in_specs=[any_spec, vmem, any_spec, vmem, any_spec, vmem, any_spec, vmem],
        out_specs=vmem,
        scratch_shapes=[
            pltpu.VMEM((n_r, rows, depth), bf16),
            pltpu.VMEM((rows, depth), bf16),
            pltpu.VMEM((4, depth, units), bf16),
            pltpu.VMEM((w_out.shape[0], depth), bf16),
            pltpu.VMEM((n_caps, features), bf16),
            pltpu.VMEM((n_r, 2, rows, units), bf16),
            pltpu.VMEM((n_r, 2, rows, units), bf16),
            pltpu.VMEM((rows, units), f32),
            pltpu.VMEM((n_r, rows, units), bf16),
            pltpu.VMEM((n_r, rows, units), bf16),
            pltpu.VMEM((n_r, rows, units), f32),
            pltpu.VMEM((n_q, 8, rows), f32),
            pltpu.VMEM((n_r, 8, rows), f32),
            pltpu.VMEM((n_q, IMAGES, units), f32),
            pltpu.VMEM((n_r, IMAGES, depth), f32),
            pltpu.VMEM((n_q, IMAGES, depth), f32),
            dma((3,)), dma((4, tiles)),
            dma((2, n_r)), dma((2, n_r + 1)), dma((n_q,)), dma((n_q,)), dma((n_r,)), dma((n_r,)),
            dma((n_r, 2, tiles)), dma((n_r, 2, tiles)), dma((n_r, tiles)), dma((n_r, tiles)),
            dma((n_q,)), dma((n_q,)), dma((n_r,)), dma((n_r,)), dma((n_q,)), dma((n_q,)),
        ],
        compiler_params=pltpu.CompilerParams(
            collective_id=0, has_side_effects=True, vmem_limit_bytes=66_000_000
        ),
        name="tower_scores",
    )(
        tokens, ln_gain, w_in, b_in[None, :], w_out, b_out[None, :], captions,
        pairs[None, :],
    )
    return result[0]


def solution(mesh):
    placed = (
        P(("group", "mrow"), ("mcol", "sub")),
        P(("mcol", "sub")),
        P(("mcol", "sub"), "mrow"),
        P("mrow"),
        P("mrow", ("mcol", "sub")),
        P(),
        P(("group", "mrow", "mcol", "sub"), None),
        P(("group", "mrow", "mcol", "sub")),
    )
    return jax.shard_map(
        functools.partial(shards, dict(mesh.shape)),
        mesh=mesh,
        in_specs=placed,
        out_specs=P(("group", "mrow", "mcol", "sub")),
        check_vma=False,
    )
```

profile of v0, /device:TPU:0, one launch (start us, length us, event | category | flops | bytes accessed | tf_op | source)
XLA Modules:
  0.0 64.7 jit_solution(3745849469948313144)
XLA Ops:
  0.0 63.5 %tower_scores.1 = f32[1,64]{1,0:T(1,128)} custom-call(bf16[128,1536]{1,0:T(8,128)(2,1)} %tokens_hbm.1, f32[1536]{0:T(1024)} %gain_ref.1, bf16[1536,6144]{1,0:T(8,128)(2,1)} %w_in_hbm.1, f32[1,6144]{1,0:T(1,128)} %bitcast.4, bf16[6144,1536]{1,0:T(8,128)(2,1)} %w_out_hbm.1, f32[1,6144]{1,0:T(1,128)} %bitcast.5, bf16[64,6144]{1,0:T(8,128)(2,1)} %captions_hbm.1, ...), custom_call_target="tpu_custom_call" | custom-call | tf_op jit(solution)/shard_map/tower_scores/pallas_call | solution.py:489
  63.5 1.2 %copy.10 = f32[64]{0:T(128)} copy(f32[64]{0:T(128)} %bitcast.7) | data formatting | bytes 512
where the time goes:
time: 64.9 us; the launch traced here: 64.7 us
  Pallas kernels  63.5 us (98%)
  local copies, waits for them, and re-layouts  1.19 us (2%)
    pallas_call x1, Pallas kernels, shards(): pl.pallas_call(functools.partial(kernel, (n_r, n_c, n_s)), out_shape=jax....  63.5 us

commit v1 on v0

v1 whole, which is shorter than its diff:
```python
import functools

import jax
import jax.numpy as jnp
from jax import lax
from jax.experimental import pallas as pl
from jax.experimental.pallas import tpu as pltpu
from jax.sharding import PartitionSpec as P

MESH = pl.DeviceIdType.MESH

D = 6144
PATCHES = 256
IMAGES = 2


def image_table(first_row, count):
    positions = first_row + jnp.arange(count, dtype=jnp.int32)
    return (positions[None, :] // PATCHES == jnp.arange(IMAGES, dtype=jnp.int32)[:, None]).astype(
        jnp.bfloat16
    )


def plain(tokens, ln_gain, w_in, b_in, w_out, b_out, captions, pairs):
    values = tokens.astype(jnp.float32)
    totals, squares = lax.psum(
        (jnp.sum(values, axis=1), jnp.sum(values * values, axis=1)), ("mcol", "sub")
    )
    average = totals / D
    variance = squares / D - average * average
    normed = (
        (values - average[:, None]) * lax.rsqrt(variance + 1e-06)[:, None] * ln_gain[None, :]
    ).astype(jnp.bfloat16)
    gathered = lax.all_gather(normed, "mrow", axis=0, tiled=True)
    rows_local = tokens.shape[0]
    columns = tokens.shape[1]
    col_index = lax.axis_index(("mcol", "sub"))
    row_index = lax.axis_index("mrow")
    resid_pool = jnp.dot(
        image_table(row_index * rows_local, rows_local), tokens, preferred_element_type=jnp.float32
    )
    empty = jnp.zeros((IMAGES, D), jnp.float32)
    offset = col_index * columns
    out_weights = w_out.astype(jnp.float32)
    full_preact = jnp.dot(gathered, w_in, preferred_element_type=jnp.float32)
    preact = lax.psum_scatter(
        full_preact.astype(jnp.bfloat16), ("mcol", "sub"), scatter_dimension=1, tiled=True
    ).astype(jnp.float32)
    units = preact.shape[1]
    unit_bias = lax.dynamic_slice_in_dim(b_in, col_index * units, units, 0)
    hidden = jax.nn.gelu(preact + unit_bias[None, :], approximate=True).astype(jnp.bfloat16)
    local_pool = jnp.dot(
        image_table(0, hidden.shape[0]), hidden, preferred_element_type=jnp.float32
    )
    pooled_hidden = lax.all_gather(local_pool, ("mcol", "sub"), axis=1, tiled=True) / PATCHES
    mixed = jnp.dot(pooled_hidden, out_weights, precision=lax.Precision.HIGHEST)
    placed = lax.dynamic_update_slice(empty, resid_pool / PATCHES + mixed, (0, offset))
    pooled = lax.psum(placed, ("mrow", "mcol", "sub")) + b_out[None, :]
    embedding = (
        pooled * lax.rsqrt(jnp.mean(pooled * pooled, axis=1, keepdims=True) + 1e-06)
    ).astype(jnp.bfloat16)
    similar = jnp.dot(captions, embedding.T, preferred_element_type=jnp.float32)
    chosen = pairs[:, None] == jnp.arange(IMAGES, dtype=jnp.int32)[None, :]
    picked = jnp.sum(jnp.where(chosen, similar, 0.0), axis=1)
    text_vals = captions.astype(jnp.float32)
    text_scale = lax.rsqrt(jnp.mean(text_vals * text_vals, axis=1) + 1e-06)
    return 100.0 * picked * text_scale / D


def column_tile(width):
    return next(t for t in (1536, 768, 512, 384, 256, 128) if width % t == 0)


def unit_tile(width):
    return next(t for t in (512, 256, 384, 128) if width % t == 0)


def kernel(
    sizes,
    tokens_hbm, gain_hbm, w_in_hbm, b_in_hbm, w_out_hbm, b_out_hbm, captions_hbm, pairs_hbm,
    out_ref,
    x_all, normed, w_in_v, w_out_v, captions_v, to_sub, from_sub, kept, to_col, from_col, own,
    gain_v, b_in_v, b_out_v, pairs_v, stats, row_stats, pool_all, acc_v, mixed_all, pooled_all,
    local_sem, w_sem,
    z_send, z_recv, stat_send, stat_recv, rows_send, rows_recv,
    sub_send, sub_recv, col_send, col_recv,
    pool_send, pool_recv, mixed_send, mixed_recv, pooled_send, pooled_recv,
):
    n_r, n_c, n_s = sizes
    n_q = n_c * n_s
    g = lax.axis_index("group")
    r = lax.axis_index("mrow")
    c = lax.axis_index("mcol")
    s = lax.axis_index("sub")
    oc, os = 1 - c, 1 - s
    q = c * n_s + s
    rows, depth = x_all.shape[1], x_all.shape[2]
    tiles, ut = own.shape[1], own.shape[3]
    units = tiles * ut
    features = depth * n_q
    n_caps = captions_v.shape[0]

    def peer_q(k):
        pc, ps = (oc if k & 2 else c), (os if k & 1 else s)
        return pc * n_s + ps, (g, r, pc, ps)

    def peer_r(k):
        other = lax.rem(r + k, n_r)
        return other, (g, other, c, s)

    quarters = (oc * n_s + os, oc * n_s + s, c * n_s + os, c * n_s + s)

    def w_in_copy(j, t):
        start = pl.multiple_of(quarters[j] * units + t * ut, 128)
        return pltpu.make_async_copy(
            w_in_hbm.at[:, pl.ds(start, ut)], w_in_v.at[j, t], w_sem.at[j, t])

    tokens_copy = pltpu.make_async_copy(tokens_hbm, x_all.at[r], local_sem.at[0])
    w_out_copy = pltpu.make_async_copy(w_out_hbm, w_out_v, local_sem.at[1])
    captions_copy = pltpu.make_async_copy(captions_hbm, captions_v, local_sem.at[2])
    gain_copy = pltpu.make_async_copy(gain_hbm, gain_v, local_sem.at[3])
    b_in_copy = pltpu.make_async_copy(
        b_in_hbm.at[:, pl.ds(pl.multiple_of(q * units, 128), units)], b_in_v, local_sem.at[4])
    b_out_copy = pltpu.make_async_copy(
        b_out_hbm.at[:, pl.ds(pl.multiple_of(q * depth, 128), depth)], b_out_v, local_sem.at[5])
    pairs_copy = pltpu.make_async_copy(pairs_hbm, pairs_v, local_sem.at[6])
    tokens_copy.start()

    barrier = pltpu.get_barrier_semaphore()
    for k in range(1, n_q):
        pl.semaphore_signal(barrier, inc=1, device_id=peer_q(k)[1], device_id_type=MESH)

    @pl.when(r > 0)
    def _():
        pl.semaphore_signal(barrier, inc=1, device_id=(g, r - 1, c, s), device_id_type=MESH)

    @pl.when(r + 1 < n_r)
    def _():
        pl.semaphore_signal(barrier, inc=1, device_id=(g, r + 1, c, s), device_id_type=MESH)

    gain_copy.start()
    tokens_copy.wait()
    for pair in (0, 2):
        for t in range(tiles):
            w_in_copy(pair, t).start()
            w_in_copy(pair + 1, t).start()
    b_in_copy.start()
    b_out_copy.start()
    pairs_copy.start()

    ct = column_tile(depth)
    total = jnp.zeros((rows, 1), jnp.float32)
    squares = jnp.zeros((rows, 1), jnp.float32)
    for start in range(0, depth, ct):
        part = x_all[r, :, start : start + ct].astype(jnp.float32)
        total += jnp.sum(part, axis=1, keepdims=True)
        squares += jnp.sum(part * part, axis=1, keepdims=True)
    lane = lax.broadcasted_iota(jnp.int32, (rows, 128), 1)
    both = jnp.where(lane == 0, total, jnp.where(lane == 1, squares, 0.0))
    stats[q] = jnp.transpose(both)[:8, :]

    neighbours = jnp.where(r > 0, 1, 0) + jnp.where(r + 1 < n_r, 1, 0)
    pl.semaphore_wait(barrier, n_q - 1 + neighbours)

    def q_copy(src, dst, send, recv, k):
        return pltpu.make_async_remote_copy(
            src_ref=src, dst_ref=dst, send_sem=send, recv_sem=recv,
            device_id=peer_q(k)[1], device_id_type=MESH)

    def stat_copy(k, slot):
        return q_copy(stats.at[slot], stats.at[slot], stat_send.at[k], stat_recv.at[k], k)

    for k in range(n_q - 1, 0, -1):
        stat_copy(k, q).start()

    def relay(ref, send, recv, way, distance, block):
        towards = r + 1 if way == 0 else r - 1
        return pltpu.make_async_remote_copy(
            src_ref=ref.at[block], dst_ref=ref.at[block], send_sem=send.at[way, distance],
            recv_sem=recv.at[way, distance + 1], device_id=(g, towards, c, s), device_id_type=MESH)

    def relay_arrival(ref, send, recv, way, distance, block):
        return pltpu.make_async_remote_copy(
            src_ref=ref.at[block], dst_ref=ref.at[block], send_sem=send.at[way, 0],
            recv_sem=recv.at[way, distance], device_id=(g, r, c, s), device_id_type=MESH)

    token_relay = (x_all, z_send, z_recv)
    rows_relay = (row_stats, rows_send, rows_recv)

    def forward(what, way, distance, block):
        @pl.when(r + 1 < n_r if way == 0 else r > 0)
        def _():
            relay(*what, way, distance, block).start()

    forward(token_relay, 0, 0, r)
    forward(token_relay, 1, 0, r)

    row_id = lax.broadcasted_iota(jnp.int32, (IMAGES, 1), 0)
    image = lax.div(r * rows, PATCHES)
    resid = jnp.sum(x_all[r].astype(jnp.float32), axis=0, keepdims=True)
    mixed_all[r] = jnp.where(row_id == image, resid, 0.0) / PATCHES

    for k in range(1, n_q):
        stat_copy(k, peer_q(k)[0]).wait_recv()
    summed = stats[0]
    for k in range(1, n_q):
        summed = summed + stats[k]
    average = summed[0:1, :] / features
    variance = summed[1:2, :] / features - average * average
    spread = lax.rsqrt(variance + 1e-06)
    first = lax.broadcasted_iota(jnp.int32, (8, rows), 0) == 0
    row_stats[r] = jnp.where(first, average, spread)
    forward(rows_relay, 0, 0, r)
    forward(rows_relay, 1, 0, r)
    gain_copy.wait()

    partner = (g, r, c, os)
    across = (g, r, oc, s)

    def sub_copy(block, half, t):
        return pltpu.make_async_remote_copy(
            src_ref=to_sub.at[block, half, t], dst_ref=from_sub.at[block, half, t],
            send_sem=sub_send.at[block, half, t], recv_sem=sub_recv.at[block, half, t],
            device_id=partner, device_id_type=MESH)

    def col_copy(block, t):
        return pltpu.make_async_remote_copy(
            src_ref=to_col.at[block, t], dst_ref=from_col.at[block, t],
            send_sem=col_send.at[block, t], recv_sem=col_recv.at[block, t],
            device_id=across, device_id_type=MESH)

    def over_tiles(width, tile, body):
        def step(i, carry):
            body(pl.ds(pl.multiple_of(i * tile, 128), tile))
            return carry

        lax.fori_loop(0, width // tile, step, 0)

    def product(j, t):
        return jnp.dot(normed[...], w_in_v[j, t], preferred_element_type=jnp.float32)

    def process(block, mine):
        columns = jnp.transpose(jnp.concatenate([row_stats[block]] * 16, axis=0))
        mean_col, spread_col = columns[:, 0:1], columns[:, 1:2]

        def normalise(cols):
            values = x_all[block, :, cols].astype(jnp.float32)
            normed[:, cols] = (
                (values - mean_col) * spread_col * gain_v[:, cols]
            ).astype(jnp.bfloat16)

        over_tiles(depth, ct, normalise)

        def ready(j, t):
            @pl.when(mine)
            def _():
                w_in_copy(j, t).wait()

        def chip_sum(t):
            sub_copy(block, 0, t).wait_recv()
            to_col[block, t] = (
                kept[t] + from_sub[block, 0, t].astype(jnp.float32)
            ).astype(jnp.bfloat16)
            col_copy(block, t).start()

        def sent_quarters(t, carry):
            ready(0, t)
            to_sub[block, 0, t] = product(0, t).astype(jnp.bfloat16)
            sub_copy(block, 0, t).start()
            ready(1, t)
            kept[t] = product(1, t)

            @pl.when(t > 0)
            def _():
                chip_sum(t - 1)

            return carry

        def own_quarters(t, carry):
            ready(2, t)
            to_sub[block, 1, t] = product(2, t).astype(jnp.bfloat16)
            sub_copy(block, 1, t).start()

            @pl.when(t == 0)
            def _():
                chip_sum(tiles - 1)

            ready(3, t)
            own[block, t] = product(3, t)
            return carry

        lax.fori_loop(0, tiles, sent_quarters, 0)
        lax.fori_loop(0, tiles, own_quarters, 0)

        @pl.when(mine)
        def _():
            w_out_copy.start()
            captions_copy.start()

    def receive(distance):
        for what in (rows_relay, token_relay):
            @pl.when(r - distance >= 0)
            def _():
                relay_arrival(*what, 0, distance, r - distance).wait_recv()
                forward(what, 0, distance, r - distance)

            @pl.when(r + distance < n_r)
            def _():
                relay_arrival(*what, 1, distance, r + distance).wait_recv()
                forward(what, 1, distance, r + distance)

    def at_distance(distance, carry):
        @pl.when(distance > 0)
        def _():
            receive(distance)

        def side(which, inner):
            block = r + distance * (2 * which - 1)
            valid = (block >= 0) & (block < n_r) & ((distance > 0) | (which == 0))

            @pl.when(valid)
            def _():
                process(block, distance == 0)

            return inner

        lax.fori_loop(0, 2, side, 0)
        return carry

    lax.fori_loop(0, n_r, at_distance, 0)

    captions_copy.wait()
    norms = jnp.zeros((n_caps, 1), jnp.float32)
    for start in range(0, features, ct):
        part = captions_v[:, start : start + ct].astype(jnp.float32)
        norms += jnp.sum(part * part, axis=1, keepdims=True)
    text_scale = lax.rsqrt(norms / features + 1e-06)
    text_row = jnp.transpose(jnp.broadcast_to(text_scale, (n_caps, 128)))[0:1, :]

    b_in_copy.wait()
    b_out_copy.wait()
    pairs_copy.wait()
    pool_all[q] = jnp.zeros((tiles, IMAGES, ut), jnp.float32)
    acc_v[...] = jnp.zeros_like(acc_v)

    def finish(block, t):
        sub_copy(block, 1, t).wait_recv()
        col_copy(block, t).wait_recv()
        v = (
            own[block, t]
            + from_sub[block, 1, t].astype(jnp.float32)
            + from_col[block, t].astype(jnp.float32)
            + b_in_v[:, pl.ds(pl.multiple_of(t * ut, 128), ut)]
        )
        inner = 0.7978845608028654 * (v + 0.044715 * (v * v * v))
        hidden = (0.5 * v * (1.0 + jnp.tanh(inner))).astype(jnp.bfloat16)
        sums = jnp.sum(hidden.astype(jnp.float32), axis=0, keepdims=True)
        image_mask = row_id == lax.div(block * rows, PATCHES)
        pool_all[q, t] += jnp.where(image_mask, sums, 0.0)

    final = jnp.where(n_r - 1 - r >= r, n_r - 1, 0)

    def finish_distance(distance, carry):
        def side(which, inner):
            block = r + distance * (2 * which - 1)
            valid = (
                (block >= 0) & (block < n_r) & ((distance > 0) | (which == 0)) & (block != final)
            )

            @pl.when(valid)
            def _():
                def body(t, inside):
                    finish(block, t)
                    return inside

                lax.fori_loop(0, tiles, body, 0)

            return inner

        lax.fori_loop(0, 2, side, 0)
        return carry

    lax.fori_loop(0, n_r, finish_distance, 0)
    w_out_copy.wait()

    def pool_copy(k, t, slot):
        return q_copy(
            pool_all.at[slot, t], pool_all.at[slot, t], pool_send.at[k, t], pool_recv.at[k, t], k)

    def mix(t):
        for k in range(n_q):
            other = peer_q(k)[0]
            if k:
                pool_copy(k, t, other).wait_recv()
            value = pool_all[other, t] / PATCHES
            high = value.astype(jnp.bfloat16).astype(jnp.float32)
            rest = value - high
            middle = rest.astype(jnp.bfloat16).astype(jnp.float32)
            low = rest - middle
            terms = jnp.concatenate(
                [high, middle, low, jnp.zeros((8 - 3 * IMAGES, ut), jnp.float32)], axis=0
            ).astype(jnp.bfloat16)
            at = pl.ds(pl.multiple_of(other * units + t * ut, 128), ut)
            acc_v[...] += jnp.dot(terms, w_out_v[at, :], preferred_element_type=jnp.float32)

    def last_block(t, carry):
        @pl.when(t < tiles)
        def _():
            finish(final, t)
            for k in range(n_q - 1, 0, -1):
                pool_copy(k, t, q).start()

        @pl.when(t > 0)
        def _():
            mix(t - 1)

        return carry

    lax.fori_loop(0, tiles + 1, last_block, 0)
    acc = acc_v[...]
    mixed_all[r] = mixed_all[r] + (
        acc[0:IMAGES] + acc[IMAGES : 2 * IMAGES] + acc[2 * IMAGES : 3 * IMAGES]
    )

    def mixed_copy(k, slot):
        return pltpu.make_async_remote_copy(
            src_ref=mixed_all.at[slot], dst_ref=mixed_all.at[slot], send_sem=mixed_send.at[k],
            recv_sem=mixed_recv.at[slot], device_id=peer_r(k)[1], device_id_type=MESH)

    for k in range(1, n_r):
        mixed_copy(k, r).start()

    for k in range(1, n_q):
        stat_copy(k, q).wait_send()

    def drain(block, carry):
        def tile(t, inner):
            sub_copy(block, 0, t).wait_send()
            sub_copy(block, 1, t).wait_send()
            col_copy(block, t).wait_send()
            return inner

        lax.fori_loop(0, tiles, tile, 0)

        for what in (rows_relay, token_relay):
            @pl.when((block <= r) & (r + 1 < n_r))
            def _():
                relay(*what, 0, r - block, block).wait_send()

            @pl.when((block >= r) & (r > 0))
            def _():
                relay(*what, 1, block - r, block).wait_send()

        return carry

    lax.fori_loop(0, n_r, drain, 0)

    for k in range(1, n_q):
        for t in range(tiles):
            pool_copy(k, t, q).wait_send()

    for k in range(1, n_r):
        mixed_copy(k, peer_r(k)[0]).wait_recv()
    pooled = b_out_v[...] + mixed_all[0]
    for k in range(1, n_r):
        pooled = pooled + mixed_all[k]
    pooled_all[q] = pooled

    def pooled_copy(k, slot):
        return q_copy(
            pooled_all.at[slot], pooled_all.at[slot], pooled_send.at[k], pooled_recv.at[k], k)

    for k in range(n_q - 1, 0, -1):
        pooled_copy(k, q).start()
    power = jnp.zeros((IMAGES, 1), jnp.float32)
    similar = jnp.zeros((8, n_caps), jnp.float32)
    for k in range(n_q):
        other = peer_q(k)[0]
        if k:
            pooled_copy(k, other).wait_recv()
        value = pooled_all[other]
        power += jnp.sum(value * value, axis=1, keepdims=True)
        high = value.astype(jnp.bfloat16).astype(jnp.float32)
        terms = jnp.concatenate(
            [high, value - high, jnp.zeros((8 - 2 * IMAGES, depth), jnp.float32)], axis=0
        ).astype(jnp.bfloat16)
        similar += lax.dot_general(
            terms, captions_v[:, pl.ds(pl.multiple_of(other * depth, 128), depth)],
            (((1,), (1,)), ((), ())), preferred_element_type=jnp.float32)
    scale = lax.rsqrt(power / features + 1e-06)
    similar = (similar[0:IMAGES] + similar[IMAGES : 2 * IMAGES]) * scale
    chosen = pairs_v[...] == lax.broadcasted_iota(jnp.int32, (IMAGES, n_caps), 0)
    picked = jnp.sum(jnp.where(chosen, similar, 0.0), axis=0, keepdims=True)
    out_ref[...] = 100.0 * picked * text_row / features

    for k in range(1, n_q):
        pooled_copy(k, q).wait_send()
    for k in range(1, n_r):
        mixed_copy(k, r).wait_send()


def shards(shape, tokens, ln_gain, w_in, b_in, w_out, b_out, captions, pairs):
    n_r, n_c, n_s = shape["mrow"], shape["mcol"], shape["sub"]
    n_q = n_c * n_s
    rows, depth = tokens.shape
    units = w_in.shape[1] // n_q
    n_caps, features = captions.shape
    fits = (
        n_c == 2 and n_s == 2 and n_r > 1 and rows % 128 == 0 and PATCHES % rows == 0
        and depth % 128 == 0 and units % 128 == 0 and n_caps % 8 == 0
        and rows * n_r == IMAGES * PATCHES
    )
    if not fits:
        return plain(tokens, ln_gain, w_in, b_in, w_out, b_out, captions, pairs)
    ut = unit_tile(units)
    tiles = units // ut
    bf16, f32 = jnp.bfloat16, jnp.float32
    any_spec = pl.BlockSpec(memory_space=pl.ANY)
    vmem = pl.BlockSpec(memory_space=pltpu.VMEM)
    dma = pltpu.SemaphoreType.DMA
    result = pl.pallas_call(
        functools.partial(kernel, (n_r, n_c, n_s)),
        out_shape=jax.ShapeDtypeStruct((1, n_caps), f32),
        in_specs=[any_spec] * 8,
        out_specs=vmem,
        scratch_shapes=[
            pltpu.VMEM((n_r, rows, depth), bf16),
            pltpu.VMEM((rows, depth), bf16),
            pltpu.VMEM((4, tiles, depth, ut), bf16),
            pltpu.VMEM((w_out.shape[0], depth), bf16),
            pltpu.VMEM((n_caps, features), bf16),
            pltpu.VMEM((n_r, 2, tiles, rows, ut), bf16),
            pltpu.VMEM((n_r, 2, tiles, rows, ut), bf16),
            pltpu.VMEM((tiles, rows, ut), f32),
            pltpu.VMEM((n_r, tiles, rows, ut), bf16),
            pltpu.VMEM((n_r, tiles, rows, ut), bf16),
            pltpu.VMEM((n_r, tiles, rows, ut), f32),
            pltpu.VMEM((1, depth), f32),
            pltpu.VMEM((1, units), f32),
            pltpu.VMEM((1, depth), f32),
            pltpu.VMEM((1, n_caps), jnp.int32),
            pltpu.VMEM((n_q, 8, rows), f32),
            pltpu.VMEM((n_r, 8, rows), f32),
            pltpu.VMEM((n_q, tiles, IMAGES, ut), f32),
            pltpu.VMEM((8, depth), f32),
            pltpu.VMEM((n_r, IMAGES, depth), f32),
            pltpu.VMEM((n_q, IMAGES, depth), f32),
            dma((7,)), dma((4, tiles)),
            dma((2, n_r)), dma((2, n_r + 1)), dma((n_q,)), dma((n_q,)),
            dma((2, n_r)), dma((2, n_r + 1)),
            dma((n_r, 2, tiles)), dma((n_r, 2, tiles)), dma((n_r, tiles)), dma((n_r, tiles)),
            dma((n_q, tiles)), dma((n_q, tiles)), dma((n_r,)), dma((n_r,)),
            dma((n_q,)), dma((n_q,)),
        ],
        compiler_params=pltpu.CompilerParams(
            collective_id=0, has_side_effects=True, vmem_limit_bytes=66_000_000
        ),
        name="tower_scores",
    )(
        tokens, ln_gain[None, :], w_in, b_in[None, :], w_out, b_out[None, :], captions,
        pairs[None, :],
    )
    return result[0]


def solution(mesh):
    placed = (
        P(("group", "mrow"), ("mcol", "sub")),
        P(("mcol", "sub")),
        P(("mcol", "sub"), "mrow"),
        P("mrow"),
        P("mrow", ("mcol", "sub")),
        P(),
        P(("group", "mrow", "mcol", "sub"), None),
        P(("group", "mrow", "mcol", "sub")),
    )
    return jax.shard_map(
        functools.partial(shards, dict(mesh.shape)),
        mesh=mesh,
        in_specs=placed,
        out_specs=P(("group", "mrow", "mcol", "sub")),
        check_vma=False,
    )
```

time: 64.9 us -> 63.9 us (0.985)
  Pallas kernels: 63.5 us -> 61.3 us
  local copies, waits for them, and re-layouts: 1.19 us -> 2.4 us
    pallas_call x1, Pallas kernels: 63.5 us -> 61.3 us  [shards(): pl.pallas_call(functools.partial(kernel, (n_r, n_c, n_s)), out_shape=jax....]
    broadcast_in_dim x0 -> x1, local copies, waits for them, and re-layouts: none -> 1.3 us  [shards(): ln_gain[None, :]]
where the time goes in v1:
time: 63.9 us; the launch traced here: 63.7 us
  Pallas kernels  61.3 us (96%)
  local copies, waits for them, and re-layouts  2.4 us (4%)
    pallas_call x1, Pallas kernels, shards(): pl.pallas_call(functools.partial(kernel, (n_r, n_c, n_s)), out_shape=jax....  61.3 us
    broadcast_in_dim x1, local copies, waits for them, and re-layouts, shards(): ln_gain[None, :]  1.3 us

profile of v1, /device:TPU:0, one launch (start us, length us, event | category | flops | bytes accessed | tf_op | source)
XLA Modules:
  0.0 63.7 jit_solution(4959571852436920291)
XLA Ops:
  0.0 1.3 %broadcast_in_dim.12.gain_hbm = f32[1,1536]{1,0:T(1,128)} reshape(f32[1536]{0:T(1024)} %param.9) | data formatting | bytes 12288 | tf_op jit(solution)/shard_map/broadcast_in_dim | solution.py:560
  1.3 61.3 %tower_scores.1 = f32[1,64]{1,0:T(1,128)} custom-call(bf16[128,1536]{1,0:T(8,128)(2,1)} %tokens_hbm.1, f32[1,1536]{1,0:T(1,128)} %broadcast_in_dim.12.gain_hbm, bf16[1536,6144]{1,0:T(8,128)(2,1)} %w_in_hbm.1, f32[1,6144]{1,0:T(1,128)} %bitcast.4, bf16[6144,1536]{1,0:T(8,128)(2,1)} %w_out_hbm.1, f32[1,6144]{1,0:T(1,128)} %bitcast.5, ...), custom_call_target="tpu_custom_call" | custom-call | tf_op jit(solution)/shard_map/tower_scores/pallas_call | solution.py:521
  62.6 1.1 %copy.10 = f32[64]{0:T(128)} copy(f32[64]{0:T(128)} %bitcast.7) | data formatting | bytes 512

commit v2 on v1

--- a/solution.py
+++ b/solution.py
@@ -79,7 +79,7 @@
     sizes,
     tokens_hbm, gain_hbm, w_in_hbm, b_in_hbm, w_out_hbm, b_out_hbm, captions_hbm, pairs_hbm,
     out_ref,
-    x_all, normed, w_in_v, w_out_v, captions_v, to_sub, from_sub, kept, to_col, from_col, own,
+    x_all, normed, w_in_v, w_out_v, captions_v, captions_t, to_sub, from_sub, kept, to_col, from_col, own,
     gain_v, b_in_v, b_out_v, pairs_v, stats, row_stats, pool_all, acc_v, mixed_all, pooled_all,
     local_sem, w_sem,
     z_send, z_recv, stat_send, stat_recv, rows_send, rows_recv,
@@ -140,13 +140,8 @@
 
     gain_copy.start()
     tokens_copy.wait()
-    for pair in (0, 2):
-        for t in range(tiles):
-            w_in_copy(pair, t).start()
-            w_in_copy(pair + 1, t).start()
-    b_in_copy.start()
-    b_out_copy.start()
-    pairs_copy.start()
+    w_in_copy(0, 0).start()
+    w_in_copy(1, 0).start()
 
     ct = column_tile(depth)
     total = jnp.zeros((rows, 1), jnp.float32)
@@ -173,27 +168,26 @@
     for k in range(n_q - 1, 0, -1):
         stat_copy(k, q).start()
 
-    def relay(ref, send, recv, way, distance, block):
-        towards = r + 1 if way == 0 else r - 1
+    half_rows = rows // 2
+
+    def relay(part, way, distance, block, to):
+        if part == 2:
+            ref, send, recv = row_stats.at[block], rows_send, rows_recv
+        else:
+            ref = x_all.at[block, pl.ds(part * half_rows, half_rows)]
+            send, recv = z_send.at[part], z_recv.at[part]
         return pltpu.make_async_remote_copy(
-            src_ref=ref.at[block], dst_ref=ref.at[block], send_sem=send.at[way, distance],
-            recv_sem=recv.at[way, distance + 1], device_id=(g, towards, c, s), device_id_type=MESH)
-
-    def relay_arrival(ref, send, recv, way, distance, block):
-        return pltpu.make_async_remote_copy(
-            src_ref=ref.at[block], dst_ref=ref.at[block], send_sem=send.at[way, 0],
-            recv_sem=recv.at[way, distance], device_id=(g, r, c, s), device_id_type=MESH)
-
-    token_relay = (x_all, z_send, z_recv)
-    rows_relay = (row_stats, rows_send, rows_recv)
-
-    def forward(what, way, distance, block):
+            src_ref=ref, dst_ref=ref, send_sem=send.at[way, distance],
+            recv_sem=recv.at[way, distance + 1], device_id=(g, to, c, s), device_id_type=MESH)
+
+    def forward(part, way, distance, block):
         @pl.when(r + 1 < n_r if way == 0 else r > 0)
         def _():
-            relay(*what, way, distance, block).start()
-
-    forward(token_relay, 0, 0, r)
-    forward(token_relay, 1, 0, r)
+            relay(part, way, distance, block, r + 1 if way == 0 else r - 1).start()
+
+    for part in (0, 1):
+        forward(part, 0, 0, r)
+        forward(part, 1, 0, r)
 
     row_id = lax.broadcasted_iota(jnp.int32, (IMAGES, 1), 0)
     image = lax.div(r * rows, PATCHES)
@@ -202,6 +196,14 @@
 
     for k in range(1, n_q):
         stat_copy(k, peer_q(k)[0]).wait_recv()
+    for pair in (0, 2):
+        for t in range(tiles):
+            if pair + t > 0:
+                w_in_copy(pair, t).start()
+                w_in_copy(pair + 1, t).start()
+    b_in_copy.start()
+    b_out_copy.start()
+    pairs_copy.start()
     summed = stats[0]
     for k in range(1, n_q):
         summed = summed + stats[k]
@@ -210,8 +212,8 @@
     spread = lax.rsqrt(variance + 1e-06)
     first = lax.broadcasted_iota(jnp.int32, (8, rows), 0) == 0
     row_stats[r] = jnp.where(first, average, spread)
-    forward(rows_relay, 0, 0, r)
-    forward(rows_relay, 1, 0, r)
+    forward(2, 0, 0, r)
+    forward(2, 1, 0, r)
     gain_copy.wait()
 
     partner = (g, r, c, os)
@@ -246,7 +248,7 @@
         def normalise(cols):
             values = x_all[block, :, cols].astype(jnp.float32)
             normed[:, cols] = (
-                (values - mean_col) * spread_col * gain_v[:, cols]
+                (values - mean_col) * spread_col * gain_v[cols][None, :]
             ).astype(jnp.bfloat16)
 
         over_tiles(depth, ct, normalise)
@@ -297,22 +299,21 @@
             w_out_copy.start()
             captions_copy.start()
 
-    def receive(distance):
-        for what in (rows_relay, token_relay):
-            @pl.when(r - distance >= 0)
-            def _():
-                relay_arrival(*what, 0, distance, r - distance).wait_recv()
-                forward(what, 0, distance, r - distance)
-
-            @pl.when(r + distance < n_r)
-            def _():
-                relay_arrival(*what, 1, distance, r + distance).wait_recv()
-                forward(what, 1, distance, r + distance)
+    def receive(part, distance):
+        @pl.when(r - distance >= 0)
+        def _():
+            relay(part, 0, distance - 1, r - distance, r).wait_recv()
+            forward(part, 0, distance, r - distance)
+
+        @pl.when(r + distance < n_r)
+        def _():
+            relay(part, 1, distance - 1, r + distance, r).wait_recv()
+            forward(part, 1, distance, r + distance)
 
     def at_distance(distance, carry):
         @pl.when(distance > 0)
         def _():
-            receive(distance)
+            receive(1, distance)
 
         def side(which, inner):
             block = r + distance * (2 * which - 1)
@@ -321,6 +322,11 @@
             @pl.when(valid)
             def _():
                 process(block, distance == 0)
+
+            @pl.when(valid & ((which == 0) | (r < distance)))
+            def _():
+                receive(2, distance + 1)
+                receive(0, distance + 1)
 
             return inner
 
@@ -334,6 +340,7 @@
     for start in range(0, features, ct):
         part = captions_v[:, start : start + ct].astype(jnp.float32)
         norms += jnp.sum(part * part, axis=1, keepdims=True)
+        captions_t[start : start + ct, :] = jnp.transpose(part).astype(jnp.bfloat16)
     text_scale = lax.rsqrt(norms / features + 1e-06)
     text_row = jnp.transpose(jnp.broadcast_to(text_scale, (n_caps, 128)))[0:1, :]
 
@@ -442,14 +449,14 @@
 
         lax.fori_loop(0, tiles, tile, 0)
 
-        for what in (rows_relay, token_relay):
+        for part in (0, 1, 2):
             @pl.when((block <= r) & (r + 1 < n_r))
             def _():
-                relay(*what, 0, r - block, block).wait_send()
+                relay(part, 0, r - block, block, r + 1).wait_send()
 
             @pl.when((block >= r) & (r > 0))
             def _():
-                relay(*what, 1, block - r, block).wait_send()
+                relay(part, 1, block - r, block, r - 1).wait_send()
 
         return carry
 
@@ -484,9 +491,9 @@
         terms = jnp.concatenate(
             [high, value - high, jnp.zeros((8 - 2 * IMAGES, depth), jnp.float32)], axis=0
         ).astype(jnp.bfloat16)
-        similar += lax.dot_general(
-            terms, captions_v[:, pl.ds(pl.multiple_of(other * depth, 128), depth)],
-            (((1,), (1,)), ((), ())), preferred_element_type=jnp.float32)
+        similar += jnp.dot(
+            terms, captions_t[pl.ds(pl.multiple_of(other * depth, 128), depth), :],
+            preferred_element_type=jnp.float32)
     scale = lax.rsqrt(power / features + 1e-06)
     similar = (similar[0:IMAGES] + similar[IMAGES : 2 * IMAGES]) * scale
     chosen = pairs_v[...] == lax.broadcasted_iota(jnp.int32, (IMAGES, n_caps), 0)
@@ -529,13 +536,14 @@
             pltpu.VMEM((4, tiles, depth, ut), bf16),
             pltpu.VMEM((w_out.shape[0], depth), bf16),
             pltpu.VMEM((n_caps, features), bf16),
+            pltpu.VMEM((features, n_caps), bf16),
             pltpu.VMEM((n_r, 2, tiles, rows, ut), bf16),
             pltpu.VMEM((n_r, 2, tiles, rows, ut), bf16),
             pltpu.VMEM((tiles, rows, ut), f32),
             pltpu.VMEM((n_r, tiles, rows, ut), bf16),
             pltpu.VMEM((n_r, tiles, rows, ut), bf16),
             pltpu.VMEM((n_r, tiles, rows, ut), f32),
-            pltpu.VMEM((1, depth), f32),
+            pltpu.VMEM((depth,), f32),
             pltpu.VMEM((1, units), f32),
             pltpu.VMEM((1, depth), f32),
             pltpu.VMEM((1, n_caps), jnp.int32),
@@ -546,7 +554,7 @@
             pltpu.VMEM((n_r, IMAGES, depth), f32),
             pltpu.VMEM((n_q, IMAGES, depth), f32),
             dma((7,)), dma((4, tiles)),
-            dma((2, n_r)), dma((2, n_r + 1)), dma((n_q,)), dma((n_q,)),
+            dma((2, 2, n_r)), dma((2, 2, n_r + 1)), dma((n_q,)), dma((n_q,)),
             dma((2, n_r)), dma((2, n_r + 1)),
             dma((n_r, 2, tiles)), dma((n_r, 2, tiles)), dma((n_r, tiles)), dma((n_r, tiles)),
             dma((n_q, tiles)), dma((n_q, tiles)), dma((n_r,)), dma((n_r,)),
@@ -557,7 +565,7 @@
         ),
         name="tower_scores",
     )(
-        tokens, ln_gain[None, :], w_in, b_in[None, :], w_out, b_out[None, :], captions,
+        tokens, ln_gain, w_in, b_in[None, :], w_out, b_out[None, :], captions,
         pairs[None, :],
     )
     return result[0]

time: 63.9 us -> 61.4 us (0.961)
  Pallas kernels: 61.3 us -> 60 us
  local copies, waits for them, and re-layouts: 2.4 us -> 1.19 us
    broadcast_in_dim x1 -> x0, local copies, waits for them, and re-layouts: 1.3 us -> none  [shards(): ln_gain[None, :]]
    pallas_call x1, Pallas kernels: 61.3 us -> 60 us  [shards(): pl.pallas_call(functools.partial(kernel, (n_r, n_c, n_s)), out_shape=jax....]
where the time goes in v2:
time: 61.4 us; the launch traced here: 61.2 us
  Pallas kernels  60 us (98%)
  local copies, waits for them, and re-layouts  1.19 us (2%)
    pallas_call x1, Pallas kernels, shards(): pl.pallas_call(functools.partial(kernel, (n_r, n_c, n_s)), out_shape=jax....  60 us

profile of v2, /device:TPU:0, one launch (start us, length us, event | category | flops | bytes accessed | tf_op | source)
XLA Modules:
  0.0 61.2 jit_solution(14124968962746503714)
XLA Ops:
  0.0 60.0 %tower_scores.1 = f32[1,64]{1,0:T(1,128)} custom-call(bf16[128,1536]{1,0:T(8,128)(2,1)} %tokens_hbm.1, f32[1536]{0:T(1024)} %gain_hbm.1, bf16[1536,6144]{1,0:T(8,128)(2,1)} %w_in_hbm.1, f32[1,6144]{1,0:T(1,128)} %bitcast.4, bf16[6144,1536]{1,0:T(8,128)(2,1)} %w_out_hbm.1, f32[1,6144]{1,0:T(1,128)} %bitcast.5, bf16[64,6144]{1,0:T(8,128)(2,1)} %captions_hbm.1, ...), custom_call_target="tpu_custom_call" | custom-call | tf_op jit(solution)/shard_map/tower_scores/pallas_call | solution.py:528
  60.0 1.2 %copy.10 = f32[64]{0:T(128)} copy(f32[64]{0:T(128)} %bitcast.7) | data formatting | bytes 512
